TPU v7x, 32 devices: a whole 2x2x4 slice. The times are simulated.
32 devices in a mesh: clip: 8 (over z, x), row: 4 (over y, core).
Axes of the slice: x: 2, y: 2, z: 4, core: 2. Of those that a mesh axis runs over, the one named last changes fastest.
Arguments:
- features: bfloat16 [8, 128, 32, 256], P('clip', None, 'row'), may hold values from -6 to 6
- out_weight: bfloat16 [3, 128, 3, 3], replicated, may hold values from -0.1875 to 0.1875
- out_bias: float32 [3], replicated, may hold values from -0.5 to 0.5
- targets: bfloat16 [8, 3, 32, 256], P('clip', None, 'row'), may hold values from -1 to 1
- weight_one: bfloat16 [64, 3, 3, 3], replicated, may hold values from -1.25 to 1.25
- bias_one: float32 [64], replicated, may hold values from -0.2 to 0.2
- weight_two: bfloat16 [64, 64, 3, 3], replicated, may hold values from -0.375 to 0.375
- bias_two: float32 [64], replicated, may hold values from -0.2 to 0.2
- weight_three: bfloat16 [128, 64, 3, 3], replicated, may hold values from -0.375 to 0.375
- bias_three: float32 [128], replicated, may hold values from -0.2 to 0.2
- weight_four: bfloat16 [128, 128, 3, 3], replicated, may hold values from -0.25 to 0.25
- bias_four: float32 [128], replicated, may hold values from -0.2 to 0.2
- lin_one: float32 [64], replicated, may hold values from 0.05 to 0.5
- lin_two: float32 [128], replicated, may hold values from 0.05 to 0.5
Outputs:
- loss: float32 [], replicated
- feature_grad: bfloat16 [8, 128, 32, 256], P('clip', None, 'row')
- out_weight_grad: float32 [3, 128, 3, 3], replicated
- out_bias_grad: float32 [3], replicated
All inputs are finite; a program needn't handle non-finite values.
Results may differ from a plain program's by a relative error of at most 0.02.
Values may be sent and summed in bfloat16 or wider, within the bound.
A program may use at most 64 MiB of HBM per device.

v0:
```python
import math
import jax
import jax.numpy as jnp
from jax import lax
from jax.sharding import PartitionSpec as P

shift_values = [-0.03, -0.088, -0.188]
scale_values = [0.458, 0.448, 0.45]


def padded_2(array, sides, width):
    for axis, dim in sides:
        size, length = (lax.axis_size(axis), array.shape[dim])
        up = [(i, (i + 1) % size) for i in range(size - 1)]
        down = [(j, i) for i, j in up]
        last = lax.slice_in_dim(array, length - width, length, axis=dim)
        leading = lax.slice_in_dim(array, 0, width, axis=dim)
        before = lax.ppermute(last, axis, up)
        after = lax.ppermute(leading, axis, down)
        array = jnp.concatenate([before, array, after], axis=dim)
    return array


def shifted(array, axis, by):
    size = lax.axis_size(axis)
    pairs = [(i, i + by) for i in range(size) if 0 <= i + by < size]
    return lax.ppermute(array, axis, pairs)


def shift_array():
    return jnp.array(shift_values, jnp.float32).reshape(1, 3, 1, 1)


def scale_array():
    return jnp.array(scale_values, jnp.float32).reshape(1, 3, 1, 1)


def gelu_exact(values):
    return values * 0.5 * (1.0 + jax.scipy.special.erf(values / math.sqrt(2.0)))


def gelu_slope(values):
    normal_cdf = 0.5 * (1.0 + jax.scipy.special.erf(values / math.sqrt(2.0)))
    density = jnp.exp(-0.5 * values * values) / math.sqrt(2.0 * math.pi)
    return normal_cdf + values * density


def pad_rows(inputs):
    return jnp.pad(inputs, ((0, 0), (0, 0), (1, 1), (0, 0)))


def flipped(weight):
    return jnp.flip(weight, (2, 3)).transpose(1, 0, 2, 3)


def conv_valid(padded, weight):
    frame_count, channels, row_total, col_count = padded.shape
    row_count = row_total - 2
    outputs = weight.shape[0]
    wide = jnp.pad(padded, ((0, 0), (0, 0), (0, 0), (1, 1)))
    total = jnp.zeros((outputs, row_count * col_count), jnp.float32)
    for row_shift in range(3):
        for col_shift in range(3):
            piece = wide[0, :, row_shift : row_shift + row_count, col_shift : col_shift + col_count]
            total = total + jnp.dot(
                weight[:, :, row_shift, col_shift],
                piece.reshape(channels, row_count * col_count),
                preferred_element_type=jnp.float32,
            )
    results = [total.reshape(outputs, row_count, col_count)]
    return jnp.stack(results)


def grad_from_output(inputs, grad_pad):
    frame_count, channels, row_count, col_count = inputs.shape
    outputs = grad_pad.shape[1]
    wide = jnp.pad(grad_pad, ((0, 0), (0, 0), (0, 0), (1, 1)))
    blocks = []
    for row_shift in range(3):
        for col_shift in range(3):
            left = wide[
                0,
                :,
                2 - row_shift : 2 - row_shift + row_count,
                2 - col_shift : 2 - col_shift + col_count,
            ].reshape(outputs, row_count * col_count)
            right = inputs[0].reshape(channels, row_count * col_count)
            total = lax.dot_general(
                left, right, (((1,), (1,)), ((), ())), preferred_element_type=jnp.float32
            )
            blocks.append(total)
    return jnp.stack(blocks).reshape(3, 3, outputs, channels).transpose(2, 3, 0, 1)


def edge_terms(row_values, kernel_row):
    col_count = row_values.shape[2]
    wide = jnp.pad(row_values, ((0, 0), (0, 0), (1, 1)))
    total = jnp.zeros((row_values.shape[0], kernel_row.shape[0], col_count), jnp.float32)
    for col_shift in range(3):
        total = total + jnp.einsum(
            "oc,fcw->fow",
            kernel_row[:, :, col_shift],
            wide[:, :, col_shift : col_shift + col_count],
            preferred_element_type=jnp.float32,
        )
    return total


def pool_mean(values):
    frame_count, channels, row_count, col_count = values.shape
    return values.reshape(frame_count, channels, row_count // 2, 2, col_count // 2, 2).mean(
        axis=(3, 5)
    )


def upsample(values):
    return jnp.repeat(jnp.repeat(values, 2, 2), 2, 3)


def vgg_forward(image, weights):
    weight_one, bias_one, weight_two, bias_two, weight_three, bias_three, weight_four, bias_four = (
        weights
    )
    image_pad = padded_2(image, (("row", 2),), 1)
    pre_one = conv_valid(image_pad, weight_one) + bias_one[None, :, None, None]
    act_one = gelu_exact(pre_one).astype(jnp.bfloat16)
    act_pad = padded_2(act_one, (("row", 2),), 1)
    pre_two = conv_valid(act_pad, weight_two) + bias_two[None, :, None, None]
    act_two = gelu_exact(pre_two)
    pooled = pool_mean(act_two).astype(jnp.bfloat16)
    pooled_pad = padded_2(pooled, (("row", 2),), 1)
    pre_three = conv_valid(pooled_pad, weight_three) + bias_three[None, :, None, None]
    act_three = gelu_exact(pre_three).astype(jnp.bfloat16)
    three_pad = padded_2(act_three, (("row", 2),), 1)
    pre_four = conv_valid(three_pad, weight_four) + bias_four[None, :, None, None]
    act_four = gelu_exact(pre_four)
    return (pre_one, pre_two, act_two, pre_three, pre_four, act_four)


def lpips_layer(feat_dec, feat_tgt, lin, count):
    norm_dec = jnp.sqrt(jnp.sum(feat_dec * feat_dec, 1, keepdims=True) + 1e-06)
    norm_tgt = jnp.sqrt(jnp.sum(feat_tgt * feat_tgt, 1, keepdims=True) + 1e-06)
    unit_dec = feat_dec / norm_dec
    differ = unit_dec - feat_tgt / norm_tgt
    scaled = lin[None, :, None, None]
    part = jnp.sum(scaled * differ * differ) / count
    grad_unit = 2.0 * scaled * differ / count
    grad_feat = (grad_unit - unit_dec * jnp.sum(grad_unit * unit_dec, 1, keepdims=True)) / norm_dec
    return (part, grad_feat)


def local(
    features,
    out_weight,
    out_bias,
    targets,
    weight_one,
    bias_one,
    weight_two,
    bias_two,
    weight_three,
    bias_three,
    weight_four,
    bias_four,
    lin_one,
    lin_two,
):
    weights = (
        weight_one,
        bias_one,
        weight_two,
        bias_two,
        weight_three,
        bias_three,
        weight_four,
        bias_four,
    )
    row_count = features.shape[2]
    width = features.shape[3]
    height = row_count * lax.axis_size("row")
    pre_out = conv_valid(pad_rows(features), out_weight)
    down_terms = edge_terms(features[:, :, row_count - 1, :], out_weight[:, :, 0, :])
    up_terms = edge_terms(features[:, :, 0, :], out_weight[:, :, 2, :])
    from_above = shifted(down_terms, "row", 1)
    from_below = shifted(up_terms, "row", -1)
    pre_out = pre_out.at[:, :, 0, :].add(from_above)
    pre_out = pre_out.at[:, :, row_count - 1, :].add(from_below)
    decoded = (pre_out + out_bias[None, :, None, None]).astype(jnp.bfloat16)
    image_dec = ((decoded.astype(jnp.float32) - shift_array()) / scale_array()).astype(jnp.bfloat16)
    image_tgt = ((targets.astype(jnp.float32) - shift_array()) / scale_array()).astype(jnp.bfloat16)
    pre_one, pre_two, act_two, pre_three, pre_four, act_four = vgg_forward(image_dec, weights)
    tgt_acts = vgg_forward(image_tgt, weights)
    part_one, grad_two = lpips_layer(act_two, tgt_acts[2], lin_one, float(height * width))
    part_two, grad_four = lpips_layer(
        act_four, tgt_acts[5], lin_two, float(height // 2 * (width // 2))
    )
    grad_pre4 = (grad_four * gelu_slope(pre_four)).astype(jnp.bfloat16)
    grad_act3 = conv_valid(padded_2(grad_pre4, (("row", 2),), 1), flipped(weight_four))
    grad_pre3 = (grad_act3 * gelu_slope(pre_three)).astype(jnp.bfloat16)
    grad_pool = conv_valid(padded_2(grad_pre3, (("row", 2),), 1), flipped(weight_three))
    grad_pre2 = ((grad_two + 0.25 * upsample(grad_pool)) * gelu_slope(pre_two)).astype(jnp.bfloat16)
    grad_act1 = conv_valid(padded_2(grad_pre2, (("row", 2),), 1), flipped(weight_two))
    grad_pre1 = (grad_act1 * gelu_slope(pre_one)).astype(jnp.bfloat16)
    grad_image = conv_valid(padded_2(grad_pre1, (("row", 2),), 1), flipped(weight_one))
    grad_dec = (grad_image / scale_array()).astype(jnp.bfloat16)
    grad_pad = padded_2(grad_dec, (("row", 2),), 1)
    feature_grad = conv_valid(grad_pad, flipped(out_weight)).astype(jnp.bfloat16)
    weight_grad = grad_from_output(features, grad_pad)
    bias_grad = jnp.sum(grad_dec.astype(jnp.float32), (0, 2, 3))
    loss, weight_total, bias_total = lax.psum(
        (part_one + part_two, weight_grad, bias_grad), ("clip", "row")
    )
    return (loss, feature_grad, weight_total, bias_total)


def solution(mesh):
    placed = (
        P("clip", None, "row", None),
        P(),
        P(),
        P("clip", None, "row", None),
        P(),
        P(),
        P(),
        P(),
        P(),
        P(),
        P(),
        P(),
        P(),
        P(),
    )
    return jax.shard_map(
        local,
        mesh=mesh,
        in_specs=placed,
        out_specs=(P(), P("clip", None, "row", None), P(), P()),
        check_vma=False,
    )
```

profile of v0, /device:TPU:0, one launch (start us, length us, event | category | flops | bytes accessed | tf_op | source)
XLA Modules:
  0.0 208.2 jit_solution(6531382458531928736)
XLA Ops:
  0.7 0.8 slice_bitcast_fusion.54
  1.4 1.4 fusion.406
  3.4 2.4 %collective-permute-start = (f32[1,3,256]{2,1,0:T(4,128)S(1)}, f32[1,3,256]{2,1,0:T(4,128)S(1)}, u32[]{:S(2)}, u32[]{:S(2)}) collective-permute-start(f32[1,3,256]{2,1,0:T(4,128)S(1)} %fusion.18), channel_id=1, source_target_pairs={{0,1},{1,2},{2,3},{4,5},{5,6},{6,7},{8,9},{9,10},{10,11},{12,13},{... | collective-permute-start | bytes 9224 | tf_op jit(solution)/shard_map/ppermute | solution.py:27
  6.4 1.3 collective-permute-start.1
  8.3 1.4 pad_slice_fusion
  11.3 0.5 broadcast_multiply_fusion
  11.8 0.8 reverse_bitcast_fusion
  14.9 0.7 reverse_bitcast_fusion.2
  15.8 5.2 %collective-permute-start.2 = (bf16[1,3,1,256]{3,1,2,0:T(4,128)(2,1)S(1)}, bf16[1,3,1,256]{3,1,2,0:T(4,128)(2,1)S(1)}, u32[]{:S(2)}, u32[]{:S(2)}) collective-permute-start(bf16[1,3,1,256]{3,1,2,0:T(4,128)(2,1)S(1)} %get-tuple-element.202), channel_id=1, source_target_pairs={{0,1},{1,2},{2,3},{4,5},{5,6},{6,7},{8,9},{9,10},{10,11},{12,13},{... | collective-permute-start | bytes 4616 | tf_op jit(solution)/shard_map/ppermute | solution.py:18
  20.9 1.3 collective-permute-start.3
  22.2 4.3 %collective-permute-start.6 = (bf16[1,3,1,256]{3,1,2,0:T(4,128)(2,1)S(1)}, bf16[1,3,1,256]{3,1,2,0:T(4,128)(2,1)S(1)}, u32[]{:S(2)}, u32[]{:S(2)}) collective-permute-start(bf16[1,3,1,256]{3,1,2,0:T(4,128)(2,1)S(1)} %get-tuple-element.198), channel_id=1, source_target_pairs={{0,1},{1,2},{2,3},{4,5},{5,6},{6,7},{8,9},{9,10},{10,11},{12,13},{... | collective-permute-start | bytes 4616 | tf_op jit(solution)/shard_map/ppermute | solution.py:18
  26.5 1.3 collective-permute-start.7
  34.3 4.3 %collective-permute-start.8 = (bf16[1,64,1,256]{3,2,1,0:T(2,128)(2,1)S(1)}, bf16[1,64,1,256]{3,2,1,0:T(2,128)(2,1)S(1)}, u32[]{:S(2)}, u32[]{:S(2)}) collective-permute-start(bf16[1,64,1,256]{3,2,1,0:T(2,128)(2,1)S(1)} %get-tuple-element.108), channel_id=1, source_target_pairs={{0,1},{1,2},{2,3},{4,5},{5,6},{6,7},{8,9},{9,10},{10,11},{12,13},{... | collective-permute-start | bytes 98312 | tf_op jit(solution)/shard_map/ppermute | solution.py:18
  38.5 1.3 collective-permute-start.9
  40.1 4.2 %collective-permute-start.4 = (bf16[1,64,1,256]{3,2,1,0:T(2,128)(2,1)S(1)}, bf16[1,64,1,256]{3,2,1,0:T(2,128)(2,1)S(1)}, u32[]{:S(2)}, u32[]{:S(2)}) collective-permute-start(bf16[1,64,1,256]{3,2,1,0:T(2,128)(2,1)S(1)} %get-tuple-element.112), channel_id=1, source_target_pairs={{0,1},{1,2},{2,3},{4,5},{5,6},{6,7},{8,9},{9,10},{10,11},{12,13},{... | collective-permute-start | bytes 98312 | tf_op jit(solution)/shard_map/ppermute | solution.py:18
  44.3 1.5 collective-permute-start.5
  46.1 2.5 %collective-permute-done.5 = bf16[1,64,1,256]{3,2,1,0:T(2,128)(2,1)S(1)} collective-permute-done((bf16[1,64,1,256]{3,2,1,0:T(2,128)(2,1)S(1)}, bf16[1,64,1,256]{3,2,1,0:T(2,128)(2,1)S(1)}, u32[]{:S(2)}, u32[]{:S(2)}) %collective-permute-start.5) | collective-permute-done | bytes 32800 | tf_op jit(solution)/shard_map/ppermute | solution.py:19
  49.5 0.8 copy-done.6
  55.1 1.2 multiply_reduce_fusion.3
  56.4 1.3 copy.255
  57.6 1.4 copy.256
  59.1 1.3 copy.252
  60.3 2.1 %copy.253 = f32[1,64,4,2,128,2]{4,1,5,3,2,0:T(8,128)} copy(f32[1,64,4,2,128,2]{1,5,4,3,2,0:T(2,128)} %bitcast.1069) | data formatting | bytes 1048576 | tf_op jit(solution)/shard_map/stack;reshape | solution.py:71
  62.5 2.1 multiply_reduce_fusion.2
  64.5 1.1 copy.350
  65.6 0.7 multiply_convert_fusion.8
  66.5 4.8 %collective-permute-start.14 = (bf16[1,64,1,128]{1,3,2,0:T(8,128)(2,1)S(1)}, bf16[1,64,1,128]{1,3,2,0:T(8,128)(2,1)S(1)}, u32[]{:S(2)}, u32[]{:S(2)}) collective-permute-start(bf16[1,64,1,128]{1,3,2,0:T(8,128)(2,1)S(1)} %get-tuple-element.172), channel_id=1, source_target_pairs={{0,1},{1,2},{2,3},{4,5},{5,6},{6,7},{8,9},{9,10},{10,11},{12,13},{... | collective-permute-start | bytes 49160 | tf_op jit(solution)/shard_map/ppermute | solution.py:18
  71.4 1.4 collective-permute-start.15
  72.8 3.0 %collective-permute-start.10 = (bf16[1,64,1,128]{1,3,2,0:T(8,128)(2,1)S(1)}, bf16[1,64,1,128]{1,3,2,0:T(8,128)(2,1)S(1)}, u32[]{:S(2)}, u32[]{:S(2)}) collective-permute-start(bf16[1,64,1,128]{1,3,2,0:T(8,128)(2,1)S(1)} %get-tuple-element.164), channel_id=1, source_target_pairs={{0,1},{1,2},{2,3},{4,5},{5,6},{6,7},{8,9},{9,10},{10,11},{12,13},{... | collective-permute-start | bytes 49160 | tf_op jit(solution)/shard_map/ppermute | solution.py:18
  75.9 1.3 collective-permute-start.11
  77.8 2.0 collective-permute-done.11
  83.6 4.5 %collective-permute-start.16 = (bf16[1,128,1,128]{1,3,2,0:T(8,128)(2,1)S(1)}, bf16[1,128,1,128]{1,3,2,0:T(8,128)(2,1)S(1)}, u32[]{:S(2)}, u32[]{:S(2)}) collective-permute-start(bf16[1,128,1,128]{1,3,2,0:T(8,128)(2,1)S(1)} %get-tuple-element.168), channel_id=1, source_target_pairs={{0,1},{1,2},{2,3},{4,5},{5,6},{6,7},{8,9},{9,10},{10,11},{12,13},{... | collective-permute-start | bytes 98312 | tf_op jit(solution)/shard_map/ppermute | solution.py:18
  88.1 1.3 collective-permute-start.17
  89.5 3.0 %collective-permute-start.12 = (bf16[1,128,1,128]{1,3,2,0:T(8,128)(2,1)S(1)}, bf16[1,128,1,128]{1,3,2,0:T(8,128)(2,1)S(1)}, u32[]{:S(2)}, u32[]{:S(2)}) collective-permute-start(bf16[1,128,1,128]{1,3,2,0:T(8,128)(2,1)S(1)} %get-tuple-element.160), channel_id=1, source_target_pairs={{0,1},{1,2},{2,3},{4,5},{5,6},{6,7},{8,9},{9,10},{10,11},{12,13},{... | collective-permute-start | bytes 98312 | tf_op jit(solution)/shard_map/ppermute | solution.py:18
  92.5 1.3 collective-permute-start.13
  95.2 1.2 collective-permute-done.13
  99.2 0.8 multiply_reduce_fusion.5
  100.4 4.7 %collective-permute-start.18 = (bf16[1,128,1,128]{1,3,2,0:T(8,128)(2,1)S(1)}, bf16[1,128,1,128]{1,3,2,0:T(8,128)(2,1)S(1)}, u32[]{:S(2)}, u32[]{:S(2)}) collective-permute-start(bf16[1,128,1,128]{1,3,2,0:T(8,128)(2,1)S(1)} %get-tuple-element.156), channel_id=1, source_target_pairs={{0,1},{1,2},{2,3},{4,5},{5,6},{6,7},{8,9},{9,10},{10,11},{12,13},{... | collective-permute-start | bytes 98312 | tf_op jit(solution)/shard_map/ppermute | solution.py:18
  105.1 1.3 collective-permute-start.19
  106.4 1.8 collective-permute-done.19
  110.4 4.1 %collective-permute-start.20 = (bf16[1,128,1,128]{1,3,2,0:T(8,128)(2,1)S(1)}, bf16[1,128,1,128]{1,3,2,0:T(8,128)(2,1)S(1)}, u32[]{:S(2)}, u32[]{:S(2)}) collective-permute-start(bf16[1,128,1,128]{1,3,2,0:T(8,128)(2,1)S(1)} %get-tuple-element.152), channel_id=1, source_target_pairs={{0,1},{1,2},{2,3},{4,5},{5,6},{6,7},{8,9},{9,10},{10,11},{12,13},{... | collective-permute-start | bytes 98312 | tf_op jit(solution)/shard_map/ppermute | solution.py:18
  114.5 1.5 collective-permute-start.21
  116.1 1.7 multiply_reduce_fusion
  117.8 1.0 copy.381
  118.7 1.0 copy.380
  119.9 0.7 copy-done.11
  122.8 1.1 copy.260
  124.0 2.0 fusion.35
  126.0 0.7 fusion.412
  126.7 3.6 %collective-permute-start.22 = (bf16[1,64,1,256]{3,2,1,0:T(2,128)(2,1)}, bf16[1,64,1,256]{3,2,1,0:T(2,128)(2,1)}, u32[]{:S(2)}, u32[]{:S(2)}) collective-permute-start(bf16[1,64,1,256]{3,2,1,0:T(2,128)(2,1)} %get-tuple-element.104), channel_id=1, source_target_pairs={{0,1},{1,2},{2,3},{4,5},{5,6},{6,7},{8,9},{9,10},{10,11},{12,13},{... | collective-permute-start | bytes 98312 | tf_op jit(solution)/shard_map/ppermute | solution.py:18
  130.4 1.3 collective-permute-start.23
  131.7 0.7 reverse_bitcast_fusion.1
  132.4 1.0 copy.262
  133.4 1.1 copy.270
  134.5 0.8 copy.261
  136.3 0.8 copy-done.12
  138.9 0.6 convolution_add_fusion.27
  141.2 3.3 %collective-permute-start.24 = (bf16[1,64,1,256]{3,2,1,0:T(2,128)(2,1)S(1)}, bf16[1,64,1,256]{3,2,1,0:T(2,128)(2,1)S(1)}, u32[]{:S(2)}, u32[]{:S(2)}) collective-permute-start(bf16[1,64,1,256]{3,2,1,0:T(2,128)(2,1)S(1)} %get-tuple-element.100), channel_id=1, source_target_pairs={{0,1},{1,2},{2,3},{4,5},{5,6},{6,7},{8,9},{9,10},{10,11},{12,13},{... | collective-permute-start | bytes 98312 | tf_op jit(solution)/shard_map/ppermute | solution.py:18
  144.5 1.3 collective-permute-start.25
  146.0 2.8 %collective-permute-done.25 = bf16[1,64,1,256]{3,2,1,0:T(2,128)(2,1)S(1)} collective-permute-done((bf16[1,64,1,256]{3,2,1,0:T(2,128)(2,1)S(1)}, bf16[1,64,1,256]{3,2,1,0:T(2,128)(2,1)S(1)}, u32[]{:S(2)}, u32[]{:S(2)}) %collective-permute-start.25) | collective-permute-done | bytes 32800 | tf_op jit(solution)/shard_map/ppermute | solution.py:19
  151.5 4.8 %collective-permute-start.26 = (bf16[1,3,1,256]{3,1,2,0:T(4,128)(2,1)S(1)}, bf16[1,3,1,256]{3,1,2,0:T(4,128)(2,1)S(1)}, u32[]{:S(2)}, u32[]{:S(2)}) collective-permute-start(bf16[1,3,1,256]{3,1,2,0:T(4,128)(2,1)S(1)} %get-tuple-element.194), channel_id=1, source_target_pairs={{0,1},{1,2},{2,3},{4,5},{5,6},{6,7},{8,9},{9,10},{10,11},{12,13},{... | collective-permute-start | bytes 4616 | tf_op jit(solution)/shard_map/ppermute | solution.py:18
  156.4 1.6 collective-permute-start.27
  162.9 1.2 copy.303
  166.7 41.5 %all-reduce.17 = (f32[]{:T(128)}, f32[3,128,3,3]{1,3,2,0:T(4,128)}, f32[3]{0:T(128)}) all-reduce(f32[]{:T(128)S(6)} %add.1136, f32[3,128,3,3]{1,3,2,0:T(4,128)S(1)} %bitcast.1222, f32[3]{0:T(128)S(1)} %get-tuple-element.57), channel_id=1, replica_groups=mesh['clip'=8,'row'=4] {'clip','row'}, use_global_device_ids=true, to_apply=%region_8.9 | all-reduce | flops 3460 | bytes 27680 | tf_op jit(solution)/shard_map/psum | solution.py:210
  (378 shorter events, 44.3 us)
Async XLA Ops:
  0.6 7.0 %copy-start.17 = (bf16[3,128,3,3]{1,3,2,0:T(4,128)(2,1)S(1)}, bf16[3,128,3,3]{1,3,2,0:T(4,128)(2,1)}, u32[]{:S(2)}) copy-start(bf16[3,128,3,3]{1,3,2,0:T(4,128)(2,1)} %param.24) | copy-start | bytes 20740
  0.6 7.1 %copy-start = (bf16[1,128,8,256]{3,2,1,0:T(8,128)(2,1)S(1)}, bf16[1,128,8,256]{3,2,1,0:T(8,128)(2,1)}, u32[]{:S(2)}) copy-start(bf16[1,128,8,256]{3,2,1,0:T(8,128)(2,1)} %param.23) | copy-start | bytes 1572868
  3.4 12.2 %collective-permute-start = (f32[1,3,256]{2,1,0:T(4,128)S(1)}, f32[1,3,256]{2,1,0:T(4,128)S(1)}, u32[]{:S(2)}, u32[]{:S(2)}) collective-permute-start(f32[1,3,256]{2,1,0:T(4,128)S(1)} %fusion.18), channel_id=1, source_target_pairs={{0,1},{1,2},{2,3},{4,5},{5,6},{6,7},{8,9},{9,10},{10,11},{12,13},{... | collective-permute-start | bytes 9224 | tf_op jit(solution)/shard_map/ppermute | solution.py:27
  6.4 9.2 %collective-permute-start.1 = (f32[1,3,256]{2,1,0:T(4,128)S(1)}, f32[1,3,256]{2,1,0:T(4,128)S(1)}, u32[]{:S(2)}, u32[]{:S(2)}) collective-permute-start(f32[1,3,256]{2,1,0:T(4,128)S(1)} %fusion.17), channel_id=1, source_target_pairs={{1,0},{2,1},{3,2},{5,4},{6,5},{7,6},{9,8},{10,9},{11,10},{13,12},{... | collective-permute-start | bytes 9224 | tf_op jit(solution)/shard_map/ppermute | solution.py:27
  10.6 0.7 copy-start.18
  10.6 0.7 copy-start.37
  10.6 1.2 copy-start.1
  10.7 1.9 copy-start.34
  14.0 0.9 copy-start.4
  14.2 1.4 copy-start.21
  14.2 1.4 copy-start.27
  14.2 1.5 copy-start.33
  14.2 1.5 copy-start.36
  15.8 12.1 %collective-permute-start.2 = (bf16[1,3,1,256]{3,1,2,0:T(4,128)(2,1)S(1)}, bf16[1,3,1,256]{3,1,2,0:T(4,128)(2,1)S(1)}, u32[]{:S(2)}, u32[]{:S(2)}) collective-permute-start(bf16[1,3,1,256]{3,1,2,0:T(4,128)(2,1)S(1)} %get-tuple-element.202), channel_id=1, source_target_pairs={{0,1},{1,2},{2,3},{4,5},{5,6},{6,7},{8,9},{9,10},{10,11},{12,13},{... | collective-permute-start | bytes 4616 | tf_op jit(solution)/shard_map/ppermute | solution.py:18
  20.9 6.9 %collective-permute-start.3 = (bf16[1,3,1,256]{3,1,2,0:T(4,128)(2,1)S(1)}, bf16[1,3,1,256]{3,1,2,0:T(4,128)(2,1)S(1)}, u32[]{:S(2)}, u32[]{:S(2)}) collective-permute-start(bf16[1,3,1,256]{3,1,2,0:T(4,128)(2,1)S(1)} %get-tuple-element.203), channel_id=1, source_target_pairs={{1,0},{2,1},{3,2},{5,4},{6,5},{7,6},{9,8},{10,9},{11,10},{13,12},{... | collective-permute-start | bytes 4616 | tf_op jit(solution)/shard_map/ppermute | solution.py:19
  22.2 8.5 %collective-permute-start.6 = (bf16[1,3,1,256]{3,1,2,0:T(4,128)(2,1)S(1)}, bf16[1,3,1,256]{3,1,2,0:T(4,128)(2,1)S(1)}, u32[]{:S(2)}, u32[]{:S(2)}) collective-permute-start(bf16[1,3,1,256]{3,1,2,0:T(4,128)(2,1)S(1)} %get-tuple-element.198), channel_id=1, source_target_pairs={{0,1},{1,2},{2,3},{4,5},{5,6},{6,7},{8,9},{9,10},{10,11},{12,13},{... | collective-permute-start | bytes 4616 | tf_op jit(solution)/shard_map/ppermute | solution.py:18
  26.5 4.3 %collective-permute-start.7 = (bf16[1,3,1,256]{3,1,2,0:T(4,128)(2,1)S(1)}, bf16[1,3,1,256]{3,1,2,0:T(4,128)(2,1)S(1)}, u32[]{:S(2)}, u32[]{:S(2)}) collective-permute-start(bf16[1,3,1,256]{3,1,2,0:T(4,128)(2,1)S(1)} %get-tuple-element.199), channel_id=1, source_target_pairs={{1,0},{2,1},{3,2},{5,4},{6,5},{7,6},{9,8},{10,9},{11,10},{13,12},{... | collective-permute-start | bytes 4616 | tf_op jit(solution)/shard_map/ppermute | solution.py:19
  33.2 0.7 copy-start.22
  34.3 11.5 %collective-permute-start.8 = (bf16[1,64,1,256]{3,2,1,0:T(2,128)(2,1)S(1)}, bf16[1,64,1,256]{3,2,1,0:T(2,128)(2,1)S(1)}, u32[]{:S(2)}, u32[]{:S(2)}) collective-permute-start(bf16[1,64,1,256]{3,2,1,0:T(2,128)(2,1)S(1)} %get-tuple-element.108), channel_id=1, source_target_pairs={{0,1},{1,2},{2,3},{4,5},{5,6},{6,7},{8,9},{9,10},{10,11},{12,13},{... | collective-permute-start | bytes 98312 | tf_op jit(solution)/shard_map/ppermute | solution.py:18
  38.5 7.2 %collective-permute-start.9 = (bf16[1,64,1,256]{3,2,1,0:T(2,128)(2,1)S(1)}, bf16[1,64,1,256]{3,2,1,0:T(2,128)(2,1)S(1)}, u32[]{:S(2)}, u32[]{:S(2)}) collective-permute-start(bf16[1,64,1,256]{3,2,1,0:T(2,128)(2,1)S(1)} %get-tuple-element.109), channel_id=1, source_target_pairs={{1,0},{2,1},{3,2},{5,4},{6,5},{7,6},{9,8},{10,9},{11,10},{13,12},{... | collective-permute-start | bytes 98312 | tf_op jit(solution)/shard_map/ppermute | solution.py:19
  40.1 6.1 %collective-permute-start.4 = (bf16[1,64,1,256]{3,2,1,0:T(2,128)(2,1)S(1)}, bf16[1,64,1,256]{3,2,1,0:T(2,128)(2,1)S(1)}, u32[]{:S(2)}, u32[]{:S(2)}) collective-permute-start(bf16[1,64,1,256]{3,2,1,0:T(2,128)(2,1)S(1)} %get-tuple-element.112), channel_id=1, source_target_pairs={{0,1},{1,2},{2,3},{4,5},{5,6},{6,7},{8,9},{9,10},{10,11},{12,13},{... | collective-permute-start | bytes 98312 | tf_op jit(solution)/shard_map/ppermute | solution.py:18
  44.3 4.4 %collective-permute-start.5 = (bf16[1,64,1,256]{3,2,1,0:T(2,128)(2,1)S(1)}, bf16[1,64,1,256]{3,2,1,0:T(2,128)(2,1)S(1)}, u32[]{:S(2)}, u32[]{:S(2)}) collective-permute-start(bf16[1,64,1,256]{3,2,1,0:T(2,128)(2,1)S(1)} %get-tuple-element.113), channel_id=1, source_target_pairs={{1,0},{2,1},{3,2},{5,4},{6,5},{7,6},{9,8},{10,9},{11,10},{13,12},{... | collective-permute-start | bytes 98312 | tf_op jit(solution)/shard_map/ppermute | solution.py:19
  49.4 0.9 copy-start.6
  64.5 1.8 copy-start.14
  66.5 10.7 %collective-permute-start.14 = (bf16[1,64,1,128]{1,3,2,0:T(8,128)(2,1)S(1)}, bf16[1,64,1,128]{1,3,2,0:T(8,128)(2,1)S(1)}, u32[]{:S(2)}, u32[]{:S(2)}) collective-permute-start(bf16[1,64,1,128]{1,3,2,0:T(8,128)(2,1)S(1)} %get-tuple-element.172), channel_id=1, source_target_pairs={{0,1},{1,2},{2,3},{4,5},{5,6},{6,7},{8,9},{9,10},{10,11},{12,13},{... | collective-permute-start | bytes 49160 | tf_op jit(solution)/shard_map/ppermute | solution.py:18
  71.4 6.0 %copy-start.5 = (bf16[128,64,3,3]{0,1,3,2:T(8,128)(2,1)S(1)}, bf16[128,64,3,3]{0,1,3,2:T(8,128)(2,1)}, u32[]{:S(2)}) copy-start(bf16[128,64,3,3]{0,1,3,2:T(8,128)(2,1)} %param.31) | copy-start | bytes 442372
  71.4 5.8 %collective-permute-start.15 = (bf16[1,64,1,128]{1,3,2,0:T(8,128)(2,1)S(1)}, bf16[1,64,1,128]{1,3,2,0:T(8,128)(2,1)S(1)}, u32[]{:S(2)}, u32[]{:S(2)}) collective-permute-start(bf16[1,64,1,128]{1,3,2,0:T(8,128)(2,1)S(1)} %get-tuple-element.173), channel_id=1, source_target_pairs={{1,0},{2,1},{3,2},{5,4},{6,5},{7,6},{9,8},{10,9},{11,10},{13,12},{... | collective-permute-start | bytes 49160 | tf_op jit(solution)/shard_map/ppermute | solution.py:19
  72.8 4.9 %collective-permute-start.10 = (bf16[1,64,1,128]{1,3,2,0:T(8,128)(2,1)S(1)}, bf16[1,64,1,128]{1,3,2,0:T(8,128)(2,1)S(1)}, u32[]{:S(2)}, u32[]{:S(2)}) collective-permute-start(bf16[1,64,1,128]{1,3,2,0:T(8,128)(2,1)S(1)} %get-tuple-element.164), channel_id=1, source_target_pairs={{0,1},{1,2},{2,3},{4,5},{5,6},{6,7},{8,9},{9,10},{10,11},{12,13},{... | collective-permute-start | bytes 49160 | tf_op jit(solution)/shard_map/ppermute | solution.py:18
  75.9 3.9 %collective-permute-start.11 = (bf16[1,64,1,128]{1,3,2,0:T(8,128)(2,1)S(1)}, bf16[1,64,1,128]{1,3,2,0:T(8,128)(2,1)S(1)}, u32[]{:S(2)}, u32[]{:S(2)}) collective-permute-start(bf16[1,64,1,128]{1,3,2,0:T(8,128)(2,1)S(1)} %get-tuple-element.165), channel_id=1, source_target_pairs={{1,0},{2,1},{3,2},{5,4},{6,5},{7,6},{9,8},{10,9},{11,10},{13,12},{... | collective-permute-start | bytes 49160 | tf_op jit(solution)/shard_map/ppermute | solution.py:19
  80.3 0.9 copy-start.16
  83.6 10.2 %collective-permute-start.16 = (bf16[1,128,1,128]{1,3,2,0:T(8,128)(2,1)S(1)}, bf16[1,128,1,128]{1,3,2,0:T(8,128)(2,1)S(1)}, u32[]{:S(2)}, u32[]{:S(2)}) collective-permute-start(bf16[1,128,1,128]{1,3,2,0:T(8,128)(2,1)S(1)} %get-tuple-element.168), channel_id=1, source_target_pairs={{0,1},{1,2},{2,3},{4,5},{5,6},{6,7},{8,9},{9,10},{10,11},{12,13},{... | collective-permute-start | bytes 98312 | tf_op jit(solution)/shard_map/ppermute | solution.py:18
  88.1 5.7 %collective-permute-start.17 = (bf16[1,128,1,128]{1,3,2,0:T(8,128)(2,1)S(1)}, bf16[1,128,1,128]{1,3,2,0:T(8,128)(2,1)S(1)}, u32[]{:S(2)}, u32[]{:S(2)}) collective-permute-start(bf16[1,128,1,128]{1,3,2,0:T(8,128)(2,1)S(1)} %get-tuple-element.169), channel_id=1, source_target_pairs={{1,0},{2,1},{3,2},{5,4},{6,5},{7,6},{9,8},{10,9},{11,10},{13,12},{... | collective-permute-start | bytes 98312 | tf_op jit(solution)/shard_map/ppermute | solution.py:19
  89.5 5.7 %collective-permute-start.12 = (bf16[1,128,1,128]{1,3,2,0:T(8,128)(2,1)S(1)}, bf16[1,128,1,128]{1,3,2,0:T(8,128)(2,1)S(1)}, u32[]{:S(2)}, u32[]{:S(2)}) collective-permute-start(bf16[1,128,1,128]{1,3,2,0:T(8,128)(2,1)S(1)} %get-tuple-element.160), channel_id=1, source_target_pairs={{0,1},{1,2},{2,3},{4,5},{5,6},{6,7},{8,9},{9,10},{10,11},{12,13},{... | collective-permute-start | bytes 98312 | tf_op jit(solution)/shard_map/ppermute | solution.py:18
  92.5 3.9 %collective-permute-start.13 = (bf16[1,128,1,128]{1,3,2,0:T(8,128)(2,1)S(1)}, bf16[1,128,1,128]{1,3,2,0:T(8,128)(2,1)S(1)}, u32[]{:S(2)}, u32[]{:S(2)}) collective-permute-start(bf16[1,128,1,128]{1,3,2,0:T(8,128)(2,1)S(1)} %get-tuple-element.161), channel_id=1, source_target_pairs={{1,0},{2,1},{3,2},{5,4},{6,5},{7,6},{9,8},{10,9},{11,10},{13,12},{... | collective-permute-start | bytes 98312 | tf_op jit(solution)/shard_map/ppermute | solution.py:19
  98.5 0.7 copy-start.32
  98.5 0.7 copy-start.38
  100.3 8.0 %copy-start.8 = (bf16[128,128,3,3]{0,1,3,2:T(8,128)(2,1)S(1)}, bf16[128,128,3,3]{0,1,3,2:T(8,128)(2,1)}, u32[]{:S(2)}) copy-start(bf16[128,128,3,3]{0,1,3,2:T(8,128)(2,1)} %reverse_bitcast_fusion) | copy-start | bytes 884740
  100.4 6.0 %collective-permute-start.18 = (bf16[1,128,1,128]{1,3,2,0:T(8,128)(2,1)S(1)}, bf16[1,128,1,128]{1,3,2,0:T(8,128)(2,1)S(1)}, u32[]{:S(2)}, u32[]{:S(2)}) collective-permute-start(bf16[1,128,1,128]{1,3,2,0:T(8,128)(2,1)S(1)} %get-tuple-element.156), channel_id=1, source_target_pairs={{0,1},{1,2},{2,3},{4,5},{5,6},{6,7},{8,9},{9,10},{10,11},{12,13},{... | collective-permute-start | bytes 98312 | tf_op jit(solution)/shard_map/ppermute | solution.py:18
  105.1 3.1 %collective-permute-start.19 = (bf16[1,128,1,128]{1,3,2,0:T(8,128)(2,1)S(1)}, bf16[1,128,1,128]{1,3,2,0:T(8,128)(2,1)S(1)}, u32[]{:S(2)}, u32[]{:S(2)}) collective-permute-start(bf16[1,128,1,128]{1,3,2,0:T(8,128)(2,1)S(1)} %get-tuple-element.157), channel_id=1, source_target_pairs={{1,0},{2,1},{3,2},{5,4},{6,5},{7,6},{9,8},{10,9},{11,10},{13,12},{... | collective-permute-start | bytes 98312 | tf_op jit(solution)/shard_map/ppermute | solution.py:19
  109.9 6.2 %copy-start.2 = (f32[64,2048]{1,0:T(8,128)S(1)}, f32[64,2048]{1,0:T(8,128)}, u32[]{:S(2)}) copy-start(f32[64,2048]{1,0:T(8,128)} %get-tuple-element.63) | copy-start | bytes 1572868
  109.9 6.2 %copy-start.25 = (f32[64]{0:T(128)S(1)}, f32[64]{0:T(128)}, u32[]{:S(2)}) copy-start(f32[64]{0:T(128)} %param.30) | copy-start | bytes 772
  109.9 6.1 %copy-start.30 = (f32[64]{0:T(128)S(1)}, f32[64]{0:T(128)}, u32[]{:S(2)}) copy-start(f32[64]{0:T(128)} %broadcast_multiply_fusion.1) | copy-start | bytes 772
  109.9 6.1 %copy-start.35 = (f32[64]{0:T(128)S(1)}, f32[64]{0:T(128)}, u32[]{:S(2)}) copy-start(f32[64]{0:T(128)} %param.35) | copy-start | bytes 772
  110.3 7.5 %copy-start.9 = (f32[512,128]{1,0:T(8,128)}, f32[512,128]{1,0:T(8,128)S(1)}, u32[]{:S(2)}) copy-start(f32[512,128]{1,0:T(8,128)S(1)} %fusion.9) | copy-start | bytes 786436
  110.4 9.3 %collective-permute-start.20 = (bf16[1,128,1,128]{1,3,2,0:T(8,128)(2,1)S(1)}, bf16[1,128,1,128]{1,3,2,0:T(8,128)(2,1)S(1)}, u32[]{:S(2)}, u32[]{:S(2)}) collective-permute-start(bf16[1,128,1,128]{1,3,2,0:T(8,128)(2,1)S(1)} %get-tuple-element.152), channel_id=1, source_target_pairs={{0,1},{1,2},{2,3},{4,5},{5,6},{6,7},{8,9},{9,10},{10,11},{12,13},{... | collective-permute-start | bytes 98312 | tf_op jit(solution)/shard_map/ppermute | solution.py:18
  114.5 5.2 %collective-permute-start.21 = (bf16[1,128,1,128]{1,3,2,0:T(8,128)(2,1)S(1)}, bf16[1,128,1,128]{1,3,2,0:T(8,128)(2,1)S(1)}, u32[]{:S(2)}, u32[]{:S(2)}) collective-permute-start(bf16[1,128,1,128]{1,3,2,0:T(8,128)(2,1)S(1)} %get-tuple-element.153), channel_id=1, source_target_pairs={{1,0},{2,1},{3,2},{5,4},{6,5},{7,6},{9,8},{10,9},{11,10},{13,12},{... | collective-permute-start | bytes 98312 | tf_op jit(solution)/shard_map/ppermute | solution.py:19
  117.7 1.9 copy-start.19
  119.7 0.9 copy-start.11
  119.9 1.4 copy-start.10
  124.0 7.7 %copy-start.7 = (bf16[64,64,3,3]{1,0,3,2:T(8,128)(2,1)S(1)}, bf16[64,64,3,3]{1,0,3,2:T(8,128)(2,1)}, u32[]{:S(2)}) copy-start(bf16[64,64,3,3]{1,0,3,2:T(8,128)(2,1)} %param.29) | copy-start | bytes 221188
  126.0 6.4 %copy-start.3 = (bf16[1,64,8,256]{3,2,1,0:T(8,128)(2,1)}, bf16[1,64,8,256]{3,2,1,0:T(8,128)(2,1)S(1)}, u32[]{:S(2)}) copy-start(bf16[1,64,8,256]{3,2,1,0:T(8,128)(2,1)S(1)} %fusion.35) | copy-start | bytes 786436
  126.7 7.8 %collective-permute-start.22 = (bf16[1,64,1,256]{3,2,1,0:T(2,128)(2,1)}, bf16[1,64,1,256]{3,2,1,0:T(2,128)(2,1)}, u32[]{:S(2)}, u32[]{:S(2)}) collective-permute-start(bf16[1,64,1,256]{3,2,1,0:T(2,128)(2,1)} %get-tuple-element.104), channel_id=1, source_target_pairs={{0,1},{1,2},{2,3},{4,5},{5,6},{6,7},{8,9},{9,10},{10,11},{12,13},{... | collective-permute-start | bytes 98312 | tf_op jit(solution)/shard_map/ppermute | solution.py:18
  130.4 5.0 %collective-permute-start.23 = (bf16[1,64,1,256]{3,2,1,0:T(2,128)(2,1)}, bf16[1,64,1,256]{3,2,1,0:T(2,128)(2,1)S(1)}, u32[]{:S(2)}, u32[]{:S(2)}) collective-permute-start(bf16[1,64,1,256]{3,2,1,0:T(2,128)(2,1)} %get-tuple-element.105), channel_id=1, source_target_pairs={{1,0},{2,1},{3,2},{5,4},{6,5},{7,6},{9,8},{10,9},{11,10},{13,12},{... | collective-permute-start | bytes 98312 | tf_op jit(solution)/shard_map/ppermute | solution.py:19
  136.2 0.9 copy-start.12
  137.6 1.0 copy-start.13
  137.7 1.2 copy-start.15
  137.7 1.2 copy-start.20
  137.7 1.2 copy-start.26
  137.7 1.2 copy-start.31
  141.2 4.8 %collective-permute-start.24 = (bf16[1,64,1,256]{3,2,1,0:T(2,128)(2,1)S(1)}, bf16[1,64,1,256]{3,2,1,0:T(2,128)(2,1)S(1)}, u32[]{:S(2)}, u32[]{:S(2)}) collective-permute-start(bf16[1,64,1,256]{3,2,1,0:T(2,128)(2,1)S(1)} %get-tuple-element.100), channel_id=1, source_target_pairs={{0,1},{1,2},{2,3},{4,5},{5,6},{6,7},{8,9},{9,10},{10,11},{12,13},{... | collective-permute-start | bytes 98312 | tf_op jit(solution)/shard_map/ppermute | solution.py:18
  144.5 4.2 %collective-permute-start.25 = (bf16[1,64,1,256]{3,2,1,0:T(2,128)(2,1)S(1)}, bf16[1,64,1,256]{3,2,1,0:T(2,128)(2,1)S(1)}, u32[]{:S(2)}, u32[]{:S(2)}) collective-permute-start(bf16[1,64,1,256]{3,2,1,0:T(2,128)(2,1)S(1)} %get-tuple-element.101), channel_id=1, source_target_pairs={{1,0},{2,1},{3,2},{5,4},{6,5},{7,6},{9,8},{10,9},{11,10},{13,12},{... | collective-permute-start | bytes 98312 | tf_op jit(solution)/shard_map/ppermute | solution.py:19
  150.3 0.9 copy-start.28
  151.5 7.7 %collective-permute-start.26 = (bf16[1,3,1,256]{3,1,2,0:T(4,128)(2,1)S(1)}, bf16[1,3,1,256]{3,1,2,0:T(4,128)(2,1)S(1)}, u32[]{:S(2)}, u32[]{:S(2)}) collective-permute-start(bf16[1,3,1,256]{3,1,2,0:T(4,128)(2,1)S(1)} %get-tuple-element.194), channel_id=1, source_target_pairs={{0,1},{1,2},{2,3},{4,5},{5,6},{6,7},{8,9},{9,10},{10,11},{12,13},{... | collective-permute-start | bytes 4616 | tf_op jit(solution)/shard_map/ppermute | solution.py:18
  156.4 3.1 %collective-permute-start.27 = (bf16[1,3,1,256]{3,1,2,0:T(4,128)(2,1)S(1)}, bf16[1,3,1,256]{3,1,2,0:T(4,128)(2,1)S(1)}, u32[]{:S(2)}, u32[]{:S(2)}) collective-permute-start(bf16[1,3,1,256]{3,1,2,0:T(4,128)(2,1)S(1)} %get-tuple-element.195), channel_id=1, source_target_pairs={{1,0},{2,1},{3,2},{5,4},{6,5},{7,6},{9,8},{10,9},{11,10},{13,12},{... | collective-permute-start | bytes 4616 | tf_op jit(solution)/shard_map/ppermute | solution.py:19
  (3 other events, 2.0 us)
where the time goes:
time: 210 us; the launch traced here: 208 us
  starting transfers between devices  75.1 us (36%)
  blocking collectives  41.5 us (20%)
  matrix products  32.7 us (16%)
  local copies, waits for them, and re-layouts  32.1 us (15%)
  other arithmetic  11.8 us (6%)
  waiting for transfers between devices  10.5 us (5%)
  between operations  4.34 us (2%)
    ppermute x13, starting transfers between devices, padded_2(): before = lax.ppermute(last, axis, up)  53.9 us
    psum x1, blocking collectives, local(): lax.psum((part_one + part_two, weight_grad, bias_grad), ('clip', 'row'))  41.5 us
    dot_general x126, matrix products, conv_valid(): jnp.dot(weight[:, :, row_shift, col_shift], piece.reshape(channels, row_c...  29.1 us
    ppermute x13, starting transfers between devices, padded_2(): after = lax.ppermute(leading, axis, down)  17.6 us
    unnamed x129, local copies, waits for them, and re-layouts  11.2 us
    ppermute x13, waiting for transfers between devices, padded_2(): after = lax.ppermute(leading, axis, down)  10.5 us
  transfers between devices with their start and end apart: 28, of which 7 were waited for; matrix products, arithmetic and copies ran while one was open for 10% of the time, Pallas kernels for 0%

commit v1 on v0

--- a/solution.py
+++ b/solution.py
@@ -6,6 +6,7 @@
 
 shift_values = [-0.03, -0.088, -0.188]
 scale_values = [0.458, 0.448, 0.45]
+_build_forms = lambda row_data: jax.lax.psum(jax.lax.psum(row_data, "row"), "clip")
 
 
 def padded_2(array, sides, width):
@@ -207,9 +208,7 @@
     feature_grad = conv_valid(grad_pad, flipped(out_weight)).astype(jnp.bfloat16)
     weight_grad = grad_from_output(features, grad_pad)
     bias_grad = jnp.sum(grad_dec.astype(jnp.float32), (0, 2, 3))
-    loss, weight_total, bias_total = lax.psum(
-        (part_one + part_two, weight_grad, bias_grad), ("clip", "row")
-    )
+    loss, weight_total, bias_total = _build_forms((part_one + part_two, weight_grad, bias_grad))
     return (loss, feature_grad, weight_total, bias_total)
 
 

time: 210 us -> 219 us (1.043)
  blocking collectives: 41.5 us -> 51.1 us
    psum x1 -> x2, blocking collectives: 41.5 us -> 51.1 us  [the longest x1 38.6 us: jax.lax.psum(jax.lax.psum(row_data, 'row'), 'clip')]
  transfers between devices with their start and end apart: 28 -> 28, of which waited for: 7 -> 7; matrix products, arithmetic and copies ran while one was open for 10% -> 9% of each run, Pallas kernels for 0% -> 0%
where the time goes in v1:
time: 219 us; the launch traced here: 218 us
  starting transfers between devices  75.1 us (34%)
  blocking collectives  51.1 us (23%)
  matrix products  32.8 us (15%)
  local copies, waits for them, and re-layouts  32.1 us (15%)
  other arithmetic  11.9 us (5%)
  waiting for transfers between devices  10.5 us (5%)
  between operations  4.42 us (2%)
    ppermute x13, starting transfers between devices, padded_2(): before = lax.ppermute(last, axis, up)  53.9 us
    psum x1, blocking collectives, jax.lax.psum(jax.lax.psum(row_data, 'row'), 'clip')  38.6 us
    dot_general x126, matrix products, conv_valid(): jnp.dot(weight[:, :, row_shift, col_shift], piece.reshape(channels, row_c...  29.1 us
    ppermute x13, starting transfers between devices, padded_2(): after = lax.ppermute(leading, axis, down)  17.6 us
    psum x1, blocking collectives, jax.lax.psum(row_data, 'row')  12.5 us
    unnamed x129, local copies, waits for them, and re-layouts  11.2 us
    ppermute x13, waiting for transfers between devices, padded_2(): after = lax.ppermute(leading, axis, down)  10.4 us
  transfers between devices with their start and end apart: 28, of which 7 were waited for; matrix products, arithmetic and copies ran while one was open for 9% of the time, Pallas kernels for 0%

profile of v1, /device:TPU:0, one launch (start us, length us, event | category | flops | bytes accessed | tf_op | source)
XLA Modules:
  0.0 217.9 jit_solution(12393790961910581182)
XLA Ops:
  0.7 0.8 slice_bitcast_fusion.54
  1.4 1.4 fusion.406
  3.4 2.4 %collective-permute-start = (f32[1,3,256]{2,1,0:T(4,128)S(1)}, f32[1,3,256]{2,1,0:T(4,128)S(1)}, u32[]{:S(2)}, u32[]{:S(2)}) collective-permute-start(f32[1,3,256]{2,1,0:T(4,128)S(1)} %fusion.18), channel_id=1, source_target_pairs={{0,1},{1,2},{2,3},{4,5},{5,6},{6,7},{8,9},{9,10},{10,11},{12,13},{... | collective-permute-start | bytes 9224 | tf_op jit(solution)/shard_map/ppermute | solution.py:28
  6.4 1.3 collective-permute-start.1
  8.3 1.4 pad_slice_fusion
  11.8 0.8 reverse_bitcast_fusion
  14.9 0.7 reverse_bitcast_fusion.2
  15.7 5.2 %collective-permute-start.2 = (bf16[1,3,1,256]{3,1,2,0:T(4,128)(2,1)S(1)}, bf16[1,3,1,256]{3,1,2,0:T(4,128)(2,1)S(1)}, u32[]{:S(2)}, u32[]{:S(2)}) collective-permute-start(bf16[1,3,1,256]{3,1,2,0:T(4,128)(2,1)S(1)} %get-tuple-element.205), channel_id=1, source_target_pairs={{0,1},{1,2},{2,3},{4,5},{5,6},{6,7},{8,9},{9,10},{10,11},{12,13},{... | collective-permute-start | bytes 4616 | tf_op jit(solution)/shard_map/ppermute | solution.py:19
  20.9 1.3 collective-permute-start.3
  22.2 4.3 %collective-permute-start.6 = (bf16[1,3,1,256]{3,1,2,0:T(4,128)(2,1)S(1)}, bf16[1,3,1,256]{3,1,2,0:T(4,128)(2,1)S(1)}, u32[]{:S(2)}, u32[]{:S(2)}) collective-permute-start(bf16[1,3,1,256]{3,1,2,0:T(4,128)(2,1)S(1)} %get-tuple-element.201), channel_id=1, source_target_pairs={{0,1},{1,2},{2,3},{4,5},{5,6},{6,7},{8,9},{9,10},{10,11},{12,13},{... | collective-permute-start | bytes 4616 | tf_op jit(solution)/shard_map/ppermute | solution.py:19
  26.5 1.3 collective-permute-start.7
  34.2 4.3 %collective-permute-start.8 = (bf16[1,64,1,256]{3,2,1,0:T(2,128)(2,1)S(1)}, bf16[1,64,1,256]{3,2,1,0:T(2,128)(2,1)S(1)}, u32[]{:S(2)}, u32[]{:S(2)}) collective-permute-start(bf16[1,64,1,256]{3,2,1,0:T(2,128)(2,1)S(1)} %get-tuple-element.111), channel_id=1, source_target_pairs={{0,1},{1,2},{2,3},{4,5},{5,6},{6,7},{8,9},{9,10},{10,11},{12,13},{... | collective-permute-start | bytes 98312 | tf_op jit(solution)/shard_map/ppermute | solution.py:19
  38.5 1.3 collective-permute-start.9
  40.0 4.2 %collective-permute-start.4 = (bf16[1,64,1,256]{3,2,1,0:T(2,128)(2,1)S(1)}, bf16[1,64,1,256]{3,2,1,0:T(2,128)(2,1)S(1)}, u32[]{:S(2)}, u32[]{:S(2)}) collective-permute-start(bf16[1,64,1,256]{3,2,1,0:T(2,128)(2,1)S(1)} %get-tuple-element.115), channel_id=1, source_target_pairs={{0,1},{1,2},{2,3},{4,5},{5,6},{6,7},{8,9},{9,10},{10,11},{12,13},{... | collective-permute-start | bytes 98312 | tf_op jit(solution)/shard_map/ppermute | solution.py:19
  44.2 1.5 collective-permute-start.5
  46.1 2.5 %collective-permute-done.5 = bf16[1,64,1,256]{3,2,1,0:T(2,128)(2,1)S(1)} collective-permute-done((bf16[1,64,1,256]{3,2,1,0:T(2,128)(2,1)S(1)}, bf16[1,64,1,256]{3,2,1,0:T(2,128)(2,1)S(1)}, u32[]{:S(2)}, u32[]{:S(2)}) %collective-permute-start.5) | collective-permute-done | bytes 32800 | tf_op jit(solution)/shard_map/ppermute | solution.py:20
  49.4 0.8 copy-done.6
  55.1 1.2 multiply_reduce_fusion.3
  56.3 1.3 copy.255
  57.6 1.4 copy.256
  59.0 1.3 copy.252
  60.3 2.1 copy.253
  62.5 2.1 multiply_reduce_fusion.2
  64.5 1.1 copy.350
  65.6 0.7 multiply_convert_fusion.8
  66.5 4.8 %collective-permute-start.14 = (bf16[1,64,1,128]{1,3,2,0:T(8,128)(2,1)S(1)}, bf16[1,64,1,128]{1,3,2,0:T(8,128)(2,1)S(1)}, u32[]{:S(2)}, u32[]{:S(2)}) collective-permute-start(bf16[1,64,1,128]{1,3,2,0:T(8,128)(2,1)S(1)} %get-tuple-element.175), channel_id=1, source_target_pairs={{0,1},{1,2},{2,3},{4,5},{5,6},{6,7},{8,9},{9,10},{10,11},{12,13},{... | collective-permute-start | bytes 49160 | tf_op jit(solution)/shard_map/ppermute | solution.py:19
  71.4 1.4 collective-permute-start.15
  72.8 3.0 %collective-permute-start.10 = (bf16[1,64,1,128]{1,3,2,0:T(8,128)(2,1)S(1)}, bf16[1,64,1,128]{1,3,2,0:T(8,128)(2,1)S(1)}, u32[]{:S(2)}, u32[]{:S(2)}) collective-permute-start(bf16[1,64,1,128]{1,3,2,0:T(8,128)(2,1)S(1)} %get-tuple-element.167), channel_id=1, source_target_pairs={{0,1},{1,2},{2,3},{4,5},{5,6},{6,7},{8,9},{9,10},{10,11},{12,13},{... | collective-permute-start | bytes 49160 | tf_op jit(solution)/shard_map/ppermute | solution.py:19
  75.9 1.3 collective-permute-start.11
  77.8 2.0 collective-permute-done.11
  83.6 4.5 %collective-permute-start.16 = (bf16[1,128,1,128]{1,3,2,0:T(8,128)(2,1)S(1)}, bf16[1,128,1,128]{1,3,2,0:T(8,128)(2,1)S(1)}, u32[]{:S(2)}, u32[]{:S(2)}) collective-permute-start(bf16[1,128,1,128]{1,3,2,0:T(8,128)(2,1)S(1)} %get-tuple-element.171), channel_id=1, source_target_pairs={{0,1},{1,2},{2,3},{4,5},{5,6},{6,7},{8,9},{9,10},{10,11},{12,13},{... | collective-permute-start | bytes 98312 | tf_op jit(solution)/shard_map/ppermute | solution.py:19
  88.1 1.3 collective-permute-start.17
  89.5 3.0 %collective-permute-start.12 = (bf16[1,128,1,128]{1,3,2,0:T(8,128)(2,1)S(1)}, bf16[1,128,1,128]{1,3,2,0:T(8,128)(2,1)S(1)}, u32[]{:S(2)}, u32[]{:S(2)}) collective-permute-start(bf16[1,128,1,128]{1,3,2,0:T(8,128)(2,1)S(1)} %get-tuple-element.163), channel_id=1, source_target_pairs={{0,1},{1,2},{2,3},{4,5},{5,6},{6,7},{8,9},{9,10},{10,11},{12,13},{... | collective-permute-start | bytes 98312 | tf_op jit(solution)/shard_map/ppermute | solution.py:19
  92.5 1.3 collective-permute-start.13
  95.2 1.2 collective-permute-done.13
  99.2 0.9 multiply_reduce_fusion.5
  100.4 4.7 %collective-permute-start.18 = (bf16[1,128,1,128]{1,3,2,0:T(8,128)(2,1)S(1)}, bf16[1,128,1,128]{1,3,2,0:T(8,128)(2,1)S(1)}, u32[]{:S(2)}, u32[]{:S(2)}) collective-permute-start(bf16[1,128,1,128]{1,3,2,0:T(8,128)(2,1)S(1)} %get-tuple-element.159), channel_id=1, source_target_pairs={{0,1},{1,2},{2,3},{4,5},{5,6},{6,7},{8,9},{9,10},{10,11},{12,13},{... | collective-permute-start | bytes 98312 | tf_op jit(solution)/shard_map/ppermute | solution.py:19
  105.1 1.3 collective-permute-start.19
  106.4 1.8 collective-permute-done.19
  110.5 4.0 %collective-permute-start.20 = (bf16[1,128,1,128]{1,3,2,0:T(8,128)(2,1)S(1)}, bf16[1,128,1,128]{1,3,2,0:T(8,128)(2,1)S(1)}, u32[]{:S(2)}, u32[]{:S(2)}) collective-permute-start(bf16[1,128,1,128]{1,3,2,0:T(8,128)(2,1)S(1)} %get-tuple-element.155), channel_id=1, source_target_pairs={{0,1},{1,2},{2,3},{4,5},{5,6},{6,7},{8,9},{9,10},{10,11},{12,13},{... | collective-permute-start | bytes 98312 | tf_op jit(solution)/shard_map/ppermute | solution.py:19
  114.6 1.5 collective-permute-start.21
  116.1 1.7 multiply_reduce_fusion
  117.8 1.0 copy.381
  118.8 1.0 copy.380
  120.0 0.7 copy-done.11
  122.9 1.1 copy.260
  124.1 2.0 fusion.35
  126.1 0.8 fusion.412
  126.8 3.7 %collective-permute-start.22 = (bf16[1,64,1,256]{3,2,1,0:T(2,128)(2,1)}, bf16[1,64,1,256]{3,2,1,0:T(2,128)(2,1)}, u32[]{:S(2)}, u32[]{:S(2)}) collective-permute-start(bf16[1,64,1,256]{3,2,1,0:T(2,128)(2,1)} %get-tuple-element.107), channel_id=1, source_target_pairs={{0,1},{1,2},{2,3},{4,5},{5,6},{6,7},{8,9},{9,10},{10,11},{12,13},{... | collective-permute-start | bytes 98312 | tf_op jit(solution)/shard_map/ppermute | solution.py:19
  130.5 1.3 collective-permute-start.23
  131.8 0.7 reverse_bitcast_fusion.1
  132.5 1.0 copy.262
  133.5 1.1 copy.270
  134.6 0.8 copy.261
  136.4 0.8 copy-done.12
  138.9 0.6 convolution_add_fusion.27
  141.2 3.3 %collective-permute-start.24 = (bf16[1,64,1,256]{3,2,1,0:T(2,128)(2,1)S(1)}, bf16[1,64,1,256]{3,2,1,0:T(2,128)(2,1)S(1)}, u32[]{:S(2)}, u32[]{:S(2)}) collective-permute-start(bf16[1,64,1,256]{3,2,1,0:T(2,128)(2,1)S(1)} %get-tuple-element.103), channel_id=1, source_target_pairs={{0,1},{1,2},{2,3},{4,5},{5,6},{6,7},{8,9},{9,10},{10,11},{12,13},{... | collective-permute-start | bytes 98312 | tf_op jit(solution)/shard_map/ppermute | solution.py:19
  144.6 1.3 collective-permute-start.25
  146.0 2.8 %collective-permute-done.25 = bf16[1,64,1,256]{3,2,1,0:T(2,128)(2,1)S(1)} collective-permute-done((bf16[1,64,1,256]{3,2,1,0:T(2,128)(2,1)S(1)}, bf16[1,64,1,256]{3,2,1,0:T(2,128)(2,1)S(1)}, u32[]{:S(2)}, u32[]{:S(2)}) %collective-permute-start.25) | collective-permute-done | bytes 32800 | tf_op jit(solution)/shard_map/ppermute | solution.py:20
  151.6 4.8 %collective-permute-start.26 = (bf16[1,3,1,256]{3,1,2,0:T(4,128)(2,1)S(1)}, bf16[1,3,1,256]{3,1,2,0:T(4,128)(2,1)S(1)}, u32[]{:S(2)}, u32[]{:S(2)}) collective-permute-start(bf16[1,3,1,256]{3,1,2,0:T(4,128)(2,1)S(1)} %get-tuple-element.197), channel_id=1, source_target_pairs={{0,1},{1,2},{2,3},{4,5},{5,6},{6,7},{8,9},{9,10},{10,11},{12,13},{... | collective-permute-start | bytes 4616 | tf_op jit(solution)/shard_map/ppermute | solution.py:19
  156.4 1.6 collective-permute-start.27
  163.0 1.2 copy.303
  166.8 12.5 %all-reduce.18 = (f32[]{:T(128)}, f32[3,128,3,3]{1,3,2,0:T(4,128)S(1)}, f32[3]{0:T(128)S(1)}) all-reduce(f32[]{:T(128)S(6)} %add.1142, f32[3,128,3,3]{1,3,2,0:T(4,128)S(1)} %bitcast.1222, f32[3]{0:T(128)S(1)} %get-tuple-element.60), channel_id=1, replica_groups=mesh['clip'=8,'row'=4] {'row'}, use_global_device_ids=true, to_apply=%region_8.9 | all-reduce | flops 3460 | bytes 27680 | tf_op jit(solution)/shard_map/psum | solution.py:9
  179.3 38.6 %all-reduce.17 = (f32[]{:T(128)}, f32[3,128,3,3]{1,3,2,0:T(4,128)}, f32[3]{0:T(128)}) all-reduce(f32[]{:T(128)} %get-tuple-element.57, f32[3,128,3,3]{1,3,2,0:T(4,128)S(1)} %get-tuple-element.58, f32[3]{0:T(128)S(1)} %get-tuple-element.59), channel_id=1, replica_groups=mesh['clip'=8,'row'=4] {'clip'}, use_global_device_ids=true, to_apply=%region_9.10 | all-reduce | flops 3460 | bytes 27680 | tf_op jit(solution)/shard_map/psum | solution.py:9
  (379 shorter events, 44.7 us)
Async XLA Ops:
  0.6 7.0 %copy-start.17 = (bf16[3,128,3,3]{1,3,2,0:T(4,128)(2,1)S(1)}, bf16[3,128,3,3]{1,3,2,0:T(4,128)(2,1)}, u32[]{:S(2)}) copy-start(bf16[3,128,3,3]{1,3,2,0:T(4,128)(2,1)} %param.24) | copy-start | bytes 20740
  0.6 7.1 %copy-start = (bf16[1,128,8,256]{3,2,1,0:T(8,128)(2,1)S(1)}, bf16[1,128,8,256]{3,2,1,0:T(8,128)(2,1)}, u32[]{:S(2)}) copy-start(bf16[1,128,8,256]{3,2,1,0:T(8,128)(2,1)} %param.23) | copy-start | bytes 1572868
  3.4 12.1 %collective-permute-start = (f32[1,3,256]{2,1,0:T(4,128)S(1)}, f32[1,3,256]{2,1,0:T(4,128)S(1)}, u32[]{:S(2)}, u32[]{:S(2)}) collective-permute-start(f32[1,3,256]{2,1,0:T(4,128)S(1)} %fusion.18), channel_id=1, source_target_pairs={{0,1},{1,2},{2,3},{4,5},{5,6},{6,7},{8,9},{9,10},{10,11},{12,13},{... | collective-permute-start | bytes 9224 | tf_op jit(solution)/shard_map/ppermute | solution.py:28
  6.4 9.2 %collective-permute-start.1 = (f32[1,3,256]{2,1,0:T(4,128)S(1)}, f32[1,3,256]{2,1,0:T(4,128)S(1)}, u32[]{:S(2)}, u32[]{:S(2)}) collective-permute-start(f32[1,3,256]{2,1,0:T(4,128)S(1)} %fusion.17), channel_id=1, source_target_pairs={{1,0},{2,1},{3,2},{5,4},{6,5},{7,6},{9,8},{10,9},{11,10},{13,12},{... | collective-permute-start | bytes 9224 | tf_op jit(solution)/shard_map/ppermute | solution.py:28
  10.5 0.7 copy-start.18
  10.5 0.7 copy-start.37
  10.6 1.2 copy-start.1
  10.7 1.8 copy-start.34
  14.0 0.9 copy-start.4
  14.2 1.4 copy-start.21
  14.2 1.4 copy-start.27
  14.2 1.4 copy-start.33
  14.2 1.4 copy-start.36
  15.7 12.1 %collective-permute-start.2 = (bf16[1,3,1,256]{3,1,2,0:T(4,128)(2,1)S(1)}, bf16[1,3,1,256]{3,1,2,0:T(4,128)(2,1)S(1)}, u32[]{:S(2)}, u32[]{:S(2)}) collective-permute-start(bf16[1,3,1,256]{3,1,2,0:T(4,128)(2,1)S(1)} %get-tuple-element.205), channel_id=1, source_target_pairs={{0,1},{1,2},{2,3},{4,5},{5,6},{6,7},{8,9},{9,10},{10,11},{12,13},{... | collective-permute-start | bytes 4616 | tf_op jit(solution)/shard_map/ppermute | solution.py:19
  20.9 6.9 %collective-permute-start.3 = (bf16[1,3,1,256]{3,1,2,0:T(4,128)(2,1)S(1)}, bf16[1,3,1,256]{3,1,2,0:T(4,128)(2,1)S(1)}, u32[]{:S(2)}, u32[]{:S(2)}) collective-permute-start(bf16[1,3,1,256]{3,1,2,0:T(4,128)(2,1)S(1)} %get-tuple-element.206), channel_id=1, source_target_pairs={{1,0},{2,1},{3,2},{5,4},{6,5},{7,6},{9,8},{10,9},{11,10},{13,12},{... | collective-permute-start | bytes 4616 | tf_op jit(solution)/shard_map/ppermute | solution.py:20
  22.2 8.5 %collective-permute-start.6 = (bf16[1,3,1,256]{3,1,2,0:T(4,128)(2,1)S(1)}, bf16[1,3,1,256]{3,1,2,0:T(4,128)(2,1)S(1)}, u32[]{:S(2)}, u32[]{:S(2)}) collective-permute-start(bf16[1,3,1,256]{3,1,2,0:T(4,128)(2,1)S(1)} %get-tuple-element.201), channel_id=1, source_target_pairs={{0,1},{1,2},{2,3},{4,5},{5,6},{6,7},{8,9},{9,10},{10,11},{12,13},{... | collective-permute-start | bytes 4616 | tf_op jit(solution)/shard_map/ppermute | solution.py:19
  26.5 4.3 %collective-permute-start.7 = (bf16[1,3,1,256]{3,1,2,0:T(4,128)(2,1)S(1)}, bf16[1,3,1,256]{3,1,2,0:T(4,128)(2,1)S(1)}, u32[]{:S(2)}, u32[]{:S(2)}) collective-permute-start(bf16[1,3,1,256]{3,1,2,0:T(4,128)(2,1)S(1)} %get-tuple-element.202), channel_id=1, source_target_pairs={{1,0},{2,1},{3,2},{5,4},{6,5},{7,6},{9,8},{10,9},{11,10},{13,12},{... | collective-permute-start | bytes 4616 | tf_op jit(solution)/shard_map/ppermute | solution.py:20
  33.2 0.7 copy-start.22
  34.2 11.5 %collective-permute-start.8 = (bf16[1,64,1,256]{3,2,1,0:T(2,128)(2,1)S(1)}, bf16[1,64,1,256]{3,2,1,0:T(2,128)(2,1)S(1)}, u32[]{:S(2)}, u32[]{:S(2)}) collective-permute-start(bf16[1,64,1,256]{3,2,1,0:T(2,128)(2,1)S(1)} %get-tuple-element.111), channel_id=1, source_target_pairs={{0,1},{1,2},{2,3},{4,5},{5,6},{6,7},{8,9},{9,10},{10,11},{12,13},{... | collective-permute-start | bytes 98312 | tf_op jit(solution)/shard_map/ppermute | solution.py:19
  38.5 7.2 %collective-permute-start.9 = (bf16[1,64,1,256]{3,2,1,0:T(2,128)(2,1)S(1)}, bf16[1,64,1,256]{3,2,1,0:T(2,128)(2,1)S(1)}, u32[]{:S(2)}, u32[]{:S(2)}) collective-permute-start(bf16[1,64,1,256]{3,2,1,0:T(2,128)(2,1)S(1)} %get-tuple-element.112), channel_id=1, source_target_pairs={{1,0},{2,1},{3,2},{5,4},{6,5},{7,6},{9,8},{10,9},{11,10},{13,12},{... | collective-permute-start | bytes 98312 | tf_op jit(solution)/shard_map/ppermute | solution.py:20
  40.0 6.1 %collective-permute-start.4 = (bf16[1,64,1,256]{3,2,1,0:T(2,128)(2,1)S(1)}, bf16[1,64,1,256]{3,2,1,0:T(2,128)(2,1)S(1)}, u32[]{:S(2)}, u32[]{:S(2)}) collective-permute-start(bf16[1,64,1,256]{3,2,1,0:T(2,128)(2,1)S(1)} %get-tuple-element.115), channel_id=1, source_target_pairs={{0,1},{1,2},{2,3},{4,5},{5,6},{6,7},{8,9},{9,10},{10,11},{12,13},{... | collective-permute-start | bytes 98312 | tf_op jit(solution)/shard_map/ppermute | solution.py:19
  44.2 4.4 %collective-permute-start.5 = (bf16[1,64,1,256]{3,2,1,0:T(2,128)(2,1)S(1)}, bf16[1,64,1,256]{3,2,1,0:T(2,128)(2,1)S(1)}, u32[]{:S(2)}, u32[]{:S(2)}) collective-permute-start(bf16[1,64,1,256]{3,2,1,0:T(2,128)(2,1)S(1)} %get-tuple-element.116), channel_id=1, source_target_pairs={{1,0},{2,1},{3,2},{5,4},{6,5},{7,6},{9,8},{10,9},{11,10},{13,12},{... | collective-permute-start | bytes 98312 | tf_op jit(solution)/shard_map/ppermute | solution.py:20
  49.3 0.9 copy-start.6
  64.5 1.8 copy-start.14
  66.5 10.7 %collective-permute-start.14 = (bf16[1,64,1,128]{1,3,2,0:T(8,128)(2,1)S(1)}, bf16[1,64,1,128]{1,3,2,0:T(8,128)(2,1)S(1)}, u32[]{:S(2)}, u32[]{:S(2)}) collective-permute-start(bf16[1,64,1,128]{1,3,2,0:T(8,128)(2,1)S(1)} %get-tuple-element.175), channel_id=1, source_target_pairs={{0,1},{1,2},{2,3},{4,5},{5,6},{6,7},{8,9},{9,10},{10,11},{12,13},{... | collective-permute-start | bytes 49160 | tf_op jit(solution)/shard_map/ppermute | solution.py:19
  71.4 6.0 %copy-start.5 = (bf16[128,64,3,3]{0,1,3,2:T(8,128)(2,1)S(1)}, bf16[128,64,3,3]{0,1,3,2:T(8,128)(2,1)}, u32[]{:S(2)}) copy-start(bf16[128,64,3,3]{0,1,3,2:T(8,128)(2,1)} %param.31) | copy-start | bytes 442372
  71.4 5.8 %collective-permute-start.15 = (bf16[1,64,1,128]{1,3,2,0:T(8,128)(2,1)S(1)}, bf16[1,64,1,128]{1,3,2,0:T(8,128)(2,1)S(1)}, u32[]{:S(2)}, u32[]{:S(2)}) collective-permute-start(bf16[1,64,1,128]{1,3,2,0:T(8,128)(2,1)S(1)} %get-tuple-element.176), channel_id=1, source_target_pairs={{1,0},{2,1},{3,2},{5,4},{6,5},{7,6},{9,8},{10,9},{11,10},{13,12},{... | collective-permute-start | bytes 49160 | tf_op jit(solution)/shard_map/ppermute | solution.py:20
  72.8 4.9 %collective-permute-start.10 = (bf16[1,64,1,128]{1,3,2,0:T(8,128)(2,1)S(1)}, bf16[1,64,1,128]{1,3,2,0:T(8,128)(2,1)S(1)}, u32[]{:S(2)}, u32[]{:S(2)}) collective-permute-start(bf16[1,64,1,128]{1,3,2,0:T(8,128)(2,1)S(1)} %get-tuple-element.167), channel_id=1, source_target_pairs={{0,1},{1,2},{2,3},{4,5},{5,6},{6,7},{8,9},{9,10},{10,11},{12,13},{... | collective-permute-start | bytes 49160 | tf_op jit(solution)/shard_map/ppermute | solution.py:19
  75.9 3.9 %collective-permute-start.11 = (bf16[1,64,1,128]{1,3,2,0:T(8,128)(2,1)S(1)}, bf16[1,64,1,128]{1,3,2,0:T(8,128)(2,1)S(1)}, u32[]{:S(2)}, u32[]{:S(2)}) collective-permute-start(bf16[1,64,1,128]{1,3,2,0:T(8,128)(2,1)S(1)} %get-tuple-element.168), channel_id=1, source_target_pairs={{1,0},{2,1},{3,2},{5,4},{6,5},{7,6},{9,8},{10,9},{11,10},{13,12},{... | collective-permute-start | bytes 49160 | tf_op jit(solution)/shard_map/ppermute | solution.py:20
  80.3 0.9 copy-start.16
  83.6 10.2 %collective-permute-start.16 = (bf16[1,128,1,128]{1,3,2,0:T(8,128)(2,1)S(1)}, bf16[1,128,1,128]{1,3,2,0:T(8,128)(2,1)S(1)}, u32[]{:S(2)}, u32[]{:S(2)}) collective-permute-start(bf16[1,128,1,128]{1,3,2,0:T(8,128)(2,1)S(1)} %get-tuple-element.171), channel_id=1, source_target_pairs={{0,1},{1,2},{2,3},{4,5},{5,6},{6,7},{8,9},{9,10},{10,11},{12,13},{... | collective-permute-start | bytes 98312 | tf_op jit(solution)/shard_map/ppermute | solution.py:19
  88.1 5.7 %collective-permute-start.17 = (bf16[1,128,1,128]{1,3,2,0:T(8,128)(2,1)S(1)}, bf16[1,128,1,128]{1,3,2,0:T(8,128)(2,1)S(1)}, u32[]{:S(2)}, u32[]{:S(2)}) collective-permute-start(bf16[1,128,1,128]{1,3,2,0:T(8,128)(2,1)S(1)} %get-tuple-element.172), channel_id=1, source_target_pairs={{1,0},{2,1},{3,2},{5,4},{6,5},{7,6},{9,8},{10,9},{11,10},{13,12},{... | collective-permute-start | bytes 98312 | tf_op jit(solution)/shard_map/ppermute | solution.py:20
  89.5 5.7 %collective-permute-start.12 = (bf16[1,128,1,128]{1,3,2,0:T(8,128)(2,1)S(1)}, bf16[1,128,1,128]{1,3,2,0:T(8,128)(2,1)S(1)}, u32[]{:S(2)}, u32[]{:S(2)}) collective-permute-start(bf16[1,128,1,128]{1,3,2,0:T(8,128)(2,1)S(1)} %get-tuple-element.163), channel_id=1, source_target_pairs={{0,1},{1,2},{2,3},{4,5},{5,6},{6,7},{8,9},{9,10},{10,11},{12,13},{... | collective-permute-start | bytes 98312 | tf_op jit(solution)/shard_map/ppermute | solution.py:19
  92.5 3.9 %collective-permute-start.13 = (bf16[1,128,1,128]{1,3,2,0:T(8,128)(2,1)S(1)}, bf16[1,128,1,128]{1,3,2,0:T(8,128)(2,1)S(1)}, u32[]{:S(2)}, u32[]{:S(2)}) collective-permute-start(bf16[1,128,1,128]{1,3,2,0:T(8,128)(2,1)S(1)} %get-tuple-element.164), channel_id=1, source_target_pairs={{1,0},{2,1},{3,2},{5,4},{6,5},{7,6},{9,8},{10,9},{11,10},{13,12},{... | collective-permute-start | bytes 98312 | tf_op jit(solution)/shard_map/ppermute | solution.py:20
  98.5 0.7 copy-start.32
  98.5 0.7 copy-start.38
  100.4 8.0 %copy-start.8 = (bf16[128,128,3,3]{0,1,3,2:T(8,128)(2,1)S(1)}, bf16[128,128,3,3]{0,1,3,2:T(8,128)(2,1)}, u32[]{:S(2)}) copy-start(bf16[128,128,3,3]{0,1,3,2:T(8,128)(2,1)} %reverse_bitcast_fusion) | copy-start | bytes 884740
  100.4 6.0 %collective-permute-start.18 = (bf16[1,128,1,128]{1,3,2,0:T(8,128)(2,1)S(1)}, bf16[1,128,1,128]{1,3,2,0:T(8,128)(2,1)S(1)}, u32[]{:S(2)}, u32[]{:S(2)}) collective-permute-start(bf16[1,128,1,128]{1,3,2,0:T(8,128)(2,1)S(1)} %get-tuple-element.159), channel_id=1, source_target_pairs={{0,1},{1,2},{2,3},{4,5},{5,6},{6,7},{8,9},{9,10},{10,11},{12,13},{... | collective-permute-start | bytes 98312 | tf_op jit(solution)/shard_map/ppermute | solution.py:19
  105.1 3.1 %collective-permute-start.19 = (bf16[1,128,1,128]{1,3,2,0:T(8,128)(2,1)S(1)}, bf16[1,128,1,128]{1,3,2,0:T(8,128)(2,1)S(1)}, u32[]{:S(2)}, u32[]{:S(2)}) collective-permute-start(bf16[1,128,1,128]{1,3,2,0:T(8,128)(2,1)S(1)} %get-tuple-element.160), channel_id=1, source_target_pairs={{1,0},{2,1},{3,2},{5,4},{6,5},{7,6},{9,8},{10,9},{11,10},{13,12},{... | collective-permute-start | bytes 98312 | tf_op jit(solution)/shard_map/ppermute | solution.py:20
  109.9 6.2 %copy-start.2 = (f32[64,2048]{1,0:T(8,128)S(1)}, f32[64,2048]{1,0:T(8,128)}, u32[]{:S(2)}) copy-start(f32[64,2048]{1,0:T(8,128)} %get-tuple-element.66) | copy-start | bytes 1572868
  109.9 6.1 %copy-start.25 = (f32[64]{0:T(128)S(1)}, f32[64]{0:T(128)}, u32[]{:S(2)}) copy-start(f32[64]{0:T(128)} %param.30) | copy-start | bytes 772
  110.0 6.1 %copy-start.30 = (f32[64]{0:T(128)S(1)}, f32[64]{0:T(128)}, u32[]{:S(2)}) copy-start(f32[64]{0:T(128)} %broadcast_multiply_fusion.1) | copy-start | bytes 772
  110.0 6.1 %copy-start.35 = (f32[64]{0:T(128)S(1)}, f32[64]{0:T(128)}, u32[]{:S(2)}) copy-start(f32[64]{0:T(128)} %param.35) | copy-start | bytes 772
  110.3 7.5 %copy-start.9 = (f32[512,128]{1,0:T(8,128)}, f32[512,128]{1,0:T(8,128)S(1)}, u32[]{:S(2)}) copy-start(f32[512,128]{1,0:T(8,128)S(1)} %fusion.9) | copy-start | bytes 786436
  110.5 9.3 %collective-permute-start.20 = (bf16[1,128,1,128]{1,3,2,0:T(8,128)(2,1)S(1)}, bf16[1,128,1,128]{1,3,2,0:T(8,128)(2,1)S(1)}, u32[]{:S(2)}, u32[]{:S(2)}) collective-permute-start(bf16[1,128,1,128]{1,3,2,0:T(8,128)(2,1)S(1)} %get-tuple-element.155), channel_id=1, source_target_pairs={{0,1},{1,2},{2,3},{4,5},{5,6},{6,7},{8,9},{9,10},{10,11},{12,13},{... | collective-permute-start | bytes 98312 | tf_op jit(solution)/shard_map/ppermute | solution.py:19
  114.6 5.2 %collective-permute-start.21 = (bf16[1,128,1,128]{1,3,2,0:T(8,128)(2,1)S(1)}, bf16[1,128,1,128]{1,3,2,0:T(8,128)(2,1)S(1)}, u32[]{:S(2)}, u32[]{:S(2)}) collective-permute-start(bf16[1,128,1,128]{1,3,2,0:T(8,128)(2,1)S(1)} %get-tuple-element.156), channel_id=1, source_target_pairs={{1,0},{2,1},{3,2},{5,4},{6,5},{7,6},{9,8},{10,9},{11,10},{13,12},{... | collective-permute-start | bytes 98312 | tf_op jit(solution)/shard_map/ppermute | solution.py:20
  117.8 2.0 copy-start.19
  119.8 0.9 copy-start.11
  120.0 1.4 copy-start.10
  124.1 7.7 %copy-start.7 = (bf16[64,64,3,3]{1,0,3,2:T(8,128)(2,1)S(1)}, bf16[64,64,3,3]{1,0,3,2:T(8,128)(2,1)}, u32[]{:S(2)}) copy-start(bf16[64,64,3,3]{1,0,3,2:T(8,128)(2,1)} %param.29) | copy-start | bytes 221188
  126.1 6.4 %copy-start.3 = (bf16[1,64,8,256]{3,2,1,0:T(8,128)(2,1)}, bf16[1,64,8,256]{3,2,1,0:T(8,128)(2,1)S(1)}, u32[]{:S(2)}) copy-start(bf16[1,64,8,256]{3,2,1,0:T(8,128)(2,1)S(1)} %fusion.35) | copy-start | bytes 786436
  126.8 7.8 %collective-permute-start.22 = (bf16[1,64,1,256]{3,2,1,0:T(2,128)(2,1)}, bf16[1,64,1,256]{3,2,1,0:T(2,128)(2,1)}, u32[]{:S(2)}, u32[]{:S(2)}) collective-permute-start(bf16[1,64,1,256]{3,2,1,0:T(2,128)(2,1)} %get-tuple-element.107), channel_id=1, source_target_pairs={{0,1},{1,2},{2,3},{4,5},{5,6},{6,7},{8,9},{9,10},{10,11},{12,13},{... | collective-permute-start | bytes 98312 | tf_op jit(solution)/shard_map/ppermute | solution.py:19
  130.5 5.0 %collective-permute-start.23 = (bf16[1,64,1,256]{3,2,1,0:T(2,128)(2,1)}, bf16[1,64,1,256]{3,2,1,0:T(2,128)(2,1)S(1)}, u32[]{:S(2)}, u32[]{:S(2)}) collective-permute-start(bf16[1,64,1,256]{3,2,1,0:T(2,128)(2,1)} %get-tuple-element.108), channel_id=1, source_target_pairs={{1,0},{2,1},{3,2},{5,4},{6,5},{7,6},{9,8},{10,9},{11,10},{13,12},{... | collective-permute-start | bytes 98312 | tf_op jit(solution)/shard_map/ppermute | solution.py:20
  136.3 0.9 copy-start.12
  137.7 1.0 copy-start.13
  137.7 1.2 copy-start.15
  137.7 1.2 copy-start.20
  137.7 1.2 copy-start.26
  137.8 1.2 copy-start.31
  141.2 4.8 %collective-permute-start.24 = (bf16[1,64,1,256]{3,2,1,0:T(2,128)(2,1)S(1)}, bf16[1,64,1,256]{3,2,1,0:T(2,128)(2,1)S(1)}, u32[]{:S(2)}, u32[]{:S(2)}) collective-permute-start(bf16[1,64,1,256]{3,2,1,0:T(2,128)(2,1)S(1)} %get-tuple-element.103), channel_id=1, source_target_pairs={{0,1},{1,2},{2,3},{4,5},{5,6},{6,7},{8,9},{9,10},{10,11},{12,13},{... | collective-permute-start | bytes 98312 | tf_op jit(solution)/shard_map/ppermute | solution.py:19
  144.6 4.2 %collective-permute-start.25 = (bf16[1,64,1,256]{3,2,1,0:T(2,128)(2,1)S(1)}, bf16[1,64,1,256]{3,2,1,0:T(2,128)(2,1)S(1)}, u32[]{:S(2)}, u32[]{:S(2)}) collective-permute-start(bf16[1,64,1,256]{3,2,1,0:T(2,128)(2,1)S(1)} %get-tuple-element.104), channel_id=1, source_target_pairs={{1,0},{2,1},{3,2},{5,4},{6,5},{7,6},{9,8},{10,9},{11,10},{13,12},{... | collective-permute-start | bytes 98312 | tf_op jit(solution)/shard_map/ppermute | solution.py:20
  150.3 0.9 copy-start.28
  151.6 7.8 %collective-permute-start.26 = (bf16[1,3,1,256]{3,1,2,0:T(4,128)(2,1)S(1)}, bf16[1,3,1,256]{3,1,2,0:T(4,128)(2,1)S(1)}, u32[]{:S(2)}, u32[]{:S(2)}) collective-permute-start(bf16[1,3,1,256]{3,1,2,0:T(4,128)(2,1)S(1)} %get-tuple-element.197), channel_id=1, source_target_pairs={{0,1},{1,2},{2,3},{4,5},{5,6},{6,7},{8,9},{9,10},{10,11},{12,13},{... | collective-permute-start | bytes 4616 | tf_op jit(solution)/shard_map/ppermute | solution.py:19
  156.4 3.1 %collective-permute-start.27 = (bf16[1,3,1,256]{3,1,2,0:T(4,128)(2,1)S(1)}, bf16[1,3,1,256]{3,1,2,0:T(4,128)(2,1)S(1)}, u32[]{:S(2)}, u32[]{:S(2)}) collective-permute-start(bf16[1,3,1,256]{3,1,2,0:T(4,128)(2,1)S(1)} %get-tuple-element.198), channel_id=1, source_target_pairs={{1,0},{2,1},{3,2},{5,4},{6,5},{7,6},{9,8},{10,9},{11,10},{13,12},{... | collective-permute-start | bytes 4616 | tf_op jit(solution)/shard_map/ppermute | solution.py:20
  (3 other events, 2.0 us)
